TPU v7x, 32 devices: a whole 2x2x4 slice. The times are simulated.
32 devices in a mesh: row: 4 (over y, core), col: 8 (over z, x).
Axes of the slice: x: 2, y: 2, z: 4, core: 2. Of those that a mesh axis runs over, the one named last changes fastest.
Arguments:
- gradient: bfloat16 [3584, 12288], P('row', 'col'), may hold values from -54 to 54
- momentum: float32 [3584, 12288], P('row', 'col'), may hold values from -54 to 54
Outputs:
- update_matrix: bfloat16 [3584, 12288], P('row', 'col')
- new_momentum: float32 [3584, 12288], P('row', 'col')
All inputs are finite; a program needn't handle non-finite values.
Results may differ from a plain program's by a relative error of at most 0.013.
Values may be sent and summed in bfloat16 or wider, within the bound.
A program may use at most 128 MiB of HBM per device.

v0:
```python
import functools
import math

import jax
import jax.numpy as jnp
from jax import lax
from jax.experimental import pallas as pl
from jax.experimental.pallas import tpu as pltpu
from jax.sharding import PartitionSpec as P

ITERS = 2

MOMENTUM_DECAY = 0.95
EPSILON = 1e-07
COEF_LINEAR = 3.4445
COEF_CUBIC = -4.775
COEF_QUINTIC = 2.0315


def outer_rows(left, right):
    return lax.dot_general(
        left, right, (((1,), (1,)), ((), ())), preferred_element_type=jnp.float32
    )


def direct_blocks(rows, block):
    if rows == 1:
        return [(0, 0, block, 0, 0)]
    half = block // 2
    middle = rows // 2
    found = []
    for j in range(rows):
        for offset in range(middle):
            i = (j + offset) % rows
            found.append((j, offset * block, block, i * block, j * block))
        low, high = min(j, (j + middle) % rows), max(j, (j + middle) % rows)
        top = low * block + (0 if j == low else half)
        found.append((j, middle * block, half, top, high * block))
    return found


def mirrored_blocks(rows):
    if rows == 1:
        return []
    middle = rows // 2
    pairs = [((j + k) % rows, j) for j in range(rows) for k in range(1, middle)]
    return pairs + [(low, low + middle) for low in range(middle)]


def chain_kernel(
    tile, factor, rows, shares_ref, x_ref, out_ref, gram_ref, first, one, two, rough, exact, total, sems
):
    size = gram_ref.shape[0]
    block = size // rows
    stride = shares_ref.shape[0] // rows
    strip = 128
    copies = []
    for number, (owner, start, height, row, column) in enumerate(direct_blocks(rows, block)):
        copies.append(
            pltpu.make_async_copy(
                shares_ref.at[pl.ds(owner * stride + start, height), :],
                gram_ref.at[pl.ds(row, height), pl.ds(column, block)],
                sems.at[number],
            )
        )
    for copy in copies:
        copy.start()
    for copy in copies:
        copy.wait()

    def squares(i, j, mirror):
        def body(step, carry):
            lanes = pl.ds(pl.multiple_of(j * block + step * strip, strip), strip)
            piece = gram_ref[pl.ds(i * block, block), lanes]
            if mirror:
                gram_ref[lanes, pl.ds(i * block, block)] = piece.T
            wide = piece.astype(jnp.float32)
            return carry + jnp.sum(wide * wide, axis=0, keepdims=True)

        return lax.fori_loop(0, block // strip, body, jnp.zeros((1, strip), jnp.float32))

    diagonal = sum(squares(i, i, False) for i in range(rows))
    others = sum(squares(i, j, True) for i, j in mirrored_blocks(rows)) + jnp.zeros_like(diagonal)
    quartic = jnp.sum(diagonal + 2.0 * others, axis=1, keepdims=True)
    scale = 1.0 / jnp.sqrt(jnp.sqrt(quartic) + EPSILON)
    square = scale * scale

    def times_gram(source, finish):
        @pl.loop(0, size // tile)
        def _(step):
            columns = pl.ds(pl.multiple_of(step * tile, tile), tile)
            value = jnp.dot(
                source[...], gram_ref[:, columns], preferred_element_type=jnp.float32
            )
            finish(columns, value * square)

    def polynomial(source, target):
        def keep(columns, value):
            exact[:, columns] = value
            rough[:, columns] = value.astype(jnp.bfloat16)

        def combine(columns, value):
            target[:, columns] = (
                COEF_LINEAR * source[:, columns].astype(jnp.float32)
                + COEF_CUBIC * exact[:, columns]
                + COEF_QUINTIC * value
            ).astype(jnp.bfloat16)

        times_gram(source, keep)
        times_gram(rough, combine)

    width = x_ref.shape[1]
    lanes_step = 128 if width % 128 == 0 else width

    @pl.loop(0, size // strip)
    def _(step):
        chunk = pl.ds(pl.multiple_of(step * strip, strip), strip)
        for lane in range(0, width, lanes_step):
            two[lane : lane + lanes_step, chunk] = x_ref[chunk, lane : lane + lanes_step].T

    polynomial(two, first)
    polynomial(first, one)
    polynomial(one, two)

    def after_product(columns, value):
        total[:, columns] = (
            COEF_LINEAR * first[:, columns].astype(jnp.float32) + COEF_CUBIC * value
        )
        one[:, columns] = value.astype(jnp.bfloat16)

    times_gram(two, after_product)
    polynomial(one, two)
    polynomial(two, one)

    def after_second(columns, value):
        two[:, columns] = (
            (total[:, columns] + COEF_QUINTIC * value) * (scale * factor)
        ).astype(jnp.bfloat16)

    times_gram(one, after_second)

    @pl.loop(0, size // strip)
    def _(step):
        chunk = pl.ds(pl.multiple_of(step * strip, strip), strip)
        for lane in range(0, width, lanes_step):
            out_ref[chunk, lane : lane + lanes_step] = two[lane : lane + lanes_step, chunk].T


def chain(shares, slab, factor, rows):
    size, width = slab.shape
    tile = 512 if size % 512 == 0 else size
    vmem = pl.BlockSpec(memory_space=pltpu.VMEM)
    half = pltpu.VMEM((width, size), jnp.bfloat16)
    full = pltpu.VMEM((width, size), jnp.float32)
    count = rows * (rows // 2 + 1)
    return pl.pallas_call(
        functools.partial(chain_kernel, tile, factor, rows),
        out_shape=jax.ShapeDtypeStruct((size, width), jnp.bfloat16),
        in_specs=[pl.BlockSpec(memory_space=pl.ANY), vmem],
        out_specs=vmem,
        scratch_shapes=[pltpu.VMEM((size, size), jnp.bfloat16)]
        + [half, half, half, half, full, full, pltpu.SemaphoreType.DMA((count,))],
        compiler_params=pltpu.CompilerParams(vmem_limit_bytes=63 * 1024 * 1024),
        name="chain",
    )(shares, slab)


def assembled(shares, rows, block):
    half = block // 2
    middle = rows // 2

    def at(i, j):
        offset = (i - j) % rows
        if offset < middle:
            return shares[j, offset * block : (offset + 1) * block]
        if offset > middle:
            return at(j, i).T
        low, high = min(i, j), max(i, j)
        value = jnp.concatenate([shares[low, -half:], shares[high, -half:]], axis=0)
        return value if i == low else value.T

    return jnp.concatenate(
        [
            jnp.concatenate([at(i, j) for j in range(rows)], axis=1)
            for i in range(rows)
        ],
        axis=0,
    )


def ring_kernel(partial_ref, out_ref, *scratch):
    landed, running, send_sems, recv_sems = scratch[:2], scratch[2:4], scratch[4], scratch[5]
    count = partial_ref.shape[0]
    column = lax.axis_index("col")
    odd, pair = lax.rem(column, 2), lax.div(column, 2)
    place = (1 - odd) * pair + odd * (count - 1 - pair)
    sign = 1 - 2 * lax.rem(lax.axis_index("row"), 2)
    ways = (sign, -sign)
    wide = landed[0].shape[2]
    lanes = (pl.ds(0, wide), pl.ds(wide, landed[1].shape[2]))

    def column_at(spot):
        spot = lax.rem(spot + 2 * count, count)
        back = lax.div(spot, count // 2)
        return (1 - back) * 2 * spot + back * (2 * (count - 1 - spot) + 1)

    barrier = pltpu.get_barrier_semaphore()
    for way in ways:
        pl.semaphore_signal(
            barrier,
            inc=1,
            device_id={"col": column_at(place + way)},
            device_id_type=pl.DeviceIdType.MESH,
        )
    pl.semaphore_wait(barrier, 2)

    def copy_of(step, k, source):
        return pltpu.make_async_remote_copy(
            src_ref=source,
            dst_ref=landed[k].at[step],
            send_sem=send_sems.at[k, step],
            recv_sem=recv_sems.at[k, step],
            device_id={"col": column_at(place + ways[k])},
            device_id_type=pl.DeviceIdType.MESH,
        )

    copies = []
    for k in range(2):
        source = partial_ref.at[column_at(place - ways[k]), :, lanes[k]]
        copies.append([copy_of(0, k, source)])
        copies[k][0].start()
    for step in range(count - 1):
        for k in range(2):
            copies[k][step].wait_recv()
            mine = partial_ref[column_at(place - ways[k] * (step + 2)), :, lanes[k]]
            value = landed[k][step].astype(jnp.float32) + mine.astype(jnp.float32)
            value = value.astype(jnp.bfloat16)
            if step < count - 2:
                running[k][step] = value
                copies[k].append(copy_of(step + 1, k, running[k].at[step]))
                copies[k][step + 1].start()
            else:
                out_ref[:, lanes[k]] = value
    for k in range(2):
        for copy in copies[k]:
            copy.wait_send()


def ring_sum(partial_value, count):
    block = partial_value.shape[1]
    height = partial_value.shape[0] // count
    wide = (block // 128 + 1) // 2 * 128
    vmem = pl.BlockSpec(memory_space=pltpu.VMEM)
    slots = [
        pltpu.VMEM((count - 1, height, width), jnp.bfloat16) for width in (wide, block - wide)
    ]
    sems = pltpu.SemaphoreType.DMA((2, count - 1))
    return pl.pallas_call(
        ring_kernel,
        out_shape=jax.ShapeDtypeStruct((height, block), jnp.bfloat16),
        in_specs=[vmem],
        out_specs=vmem,
        scratch_shapes=slots + slots + [sems, sems],
        compiler_params=pltpu.CompilerParams(
            collective_id=0, has_side_effects=True, vmem_limit_bytes=40 * 1024 * 1024
        ),
        name="ring_sum",
    )(partial_value.reshape(count, height, block))


def per_device(factor, gradient, momentum):
    rows = lax.axis_size("row")
    grad32 = gradient.astype(jnp.float32)
    buffer = MOMENTUM_DECAY * momentum + grad32
    nesterov = grad32 + MOMENTUM_DECAY * buffer
    base = nesterov.astype(jnp.bfloat16)
    block = base.shape[0]
    half = block // 2
    middle = rows // 2
    me = lax.axis_index("row")
    panel = lax.all_gather(base, "row", axis=0, tiled=True)

    def rows_of(offset):
        start = ((me + offset) % rows) * block
        return lax.dynamic_slice_in_dim(panel, start, block, axis=0)

    parts = [outer_rows(base, base)]
    for offset in range(1, middle):
        parts.append(outer_rows(rows_of(offset), base))
    facing = rows_of(middle)
    lower = me < middle
    parts.append(
        outer_rows(
            jnp.where(lower, base[:half], facing[half:]), jnp.where(lower, facing, base)
        )
    )
    partial_value = jnp.concatenate([part.astype(jnp.bfloat16) for part in parts], axis=0)
    count = lax.axis_size("col")
    if block % 128 or count % 2 or count < 4:
        share = lax.psum_scatter(partial_value, "col", scatter_dimension=0, tiled=True)
    else:
        share = ring_sum(partial_value, count)
    shares = lax.all_gather(share, ("row", "col"), axis=0, tiled=True)
    parts = rows
    if block % 128:
        shares = assembled(shares.reshape(rows, -1, block), rows, block)
        parts = 1

    width = panel.shape[1] // rows
    slab = lax.dynamic_slice_in_dim(panel, me * width, width, axis=1)
    update = chain(shares, slab, factor, parts)
    update = lax.all_to_all(update, "row", 0, 1, tiled=True)
    return (update, buffer)


def solution(mesh):
    def whole(gradient, momentum):
        factor = 0.2 * math.sqrt(max(gradient.shape))
        return jax.shard_map(
            functools.partial(per_device, factor),
            mesh=mesh,
            in_specs=(P("row", "col"), P("row", "col")),
            out_specs=(P("row", "col"), P("row", "col")),
            check_vma=False,
        )(gradient, momentum)

    return whole
```

profile of v0, /device:TPU:0, one launch (start us, length us, event | category | flops | bytes accessed | tf_op | source)
XLA Modules:
  0.0 473.8 jit_solution(3291761606591850008)
XLA Ops:
  7.2 0.0 all-gather.3.cloned.1.call-start
  7.2 7.9 %fusion = (bf16[896,1536]{1,0:T(8,128)(2,1)}, f32[896,1536]{1,0:T(8,128)}) fusion(bf16[896,1536]{1,0:T(8,128)(2,1)} %param.2, f32[896,1536]{1,0:T(8,128)} %param.3), kind=kLoop, calls=%fused_computation.2 | loop fusion | flops 8257536 | bytes 16515072 | tf_op jit(solution)/shard_map/convert_element_type | solution.py:276
  15.1 0.0 copy-start
  15.1 0.0 all-gather.3.cloned.1.call-update
  15.1 0.0 all-gather.5.cloned.1.call-start
  15.2 1.7 copy-done
  16.9 4.2 convolution_convert_fusion
  21.0 70.1 %all-gather.3.cloned.1.call-done = bf16[3584,1536]{1,0:T(8,128)(2,1)} async-done(((bf16[896,1536]{1,0:T(8,128)(2,1)}), bf16[3584,1536]{1,0:T(8,128)(2,1)}) %all-gather.3.cloned.1.call-update) | async-done | bytes 11010064 | tf_op jit(solution)/shard_map/all_gather | solution.py:281
  91.2 4.8 %fusion.7 = bf16[896,896]{1,0:T(8,128)(2,1)S(1)} fusion(bf16[896,1536]{1,0:T(8,128)(2,1)S(1)} %copy-done, bf16[3584,1536]{1,0:T(8,128)(2,1)} %all-gather.3.cloned.1.call-done, s32[]{:T(128)S(6)} %select_n.37), kind=kOutput, calls=%fused_computation.11 | convolution fusion | flops 2467053568 | bytes 7110660 | tf_op jit(solution)/shard_map/dot_general | solution.py:21
  96.0 0.0 copy-start.1
  96.0 3.9 fusion.10
  99.9 0.0 copy-done.1
  99.9 7.5 %pad_maximum_fusion = bf16[2240,896]{1,0:T(8,128)(2,1)S(1)} fusion(bf16[448,896]{1,0:T(8,128)(2,1)S(1)} %fusion.10, bf16[896,896]{1,0:T(8,128)(2,1)S(1)} %fusion.7, bf16[896,896]{1,0:T(8,128)(2,1)S(1)} %copy-done.1), kind=kLoop, calls=%fused_computation.3 | loop fusion | flops 12042240 | bytes 8028160 | tf_op jit(solution)/shard_map/concatenate | solution.py:297
  107.5 55.3 %ring_sum.1 = bf16[280,896]{1,0:T(8,128)(2,1)} custom-call(bf16[8,280,896]{2,1,0:T(8,128)(2,1)S(1)} %bitcast.8), custom_call_target="tpu_custom_call" | custom-call | tf_op jit(solution)/shard_map/ring_sum/pallas_call | solution.py:258
  162.8 0.0 all-gather.5.cloned.1.call-update
  162.8 3.6 constant_dynamic-slice_fusion.x_ref
  166.4 105.0 %all-gather.5.cloned.1.call-done.shares_ref = bf16[8960,896]{1,0:T(8,128)(2,1)} async-done(((bf16[280,896]{1,0:T(8,128)(2,1)}), bf16[8960,896]{1,0:T(8,128)(2,1)}) %all-gather.5.cloned.1.call-update) | async-done | bytes 16056336 | tf_op jit(solution)/shard_map/all_gather | solution.py:303
  271.4 157.5 %chain.1 = bf16[3584,384]{1,0:T(8,128)(2,1)} custom-call(bf16[8960,896]{1,0:T(8,128)(2,1)} %all-gather.5.cloned.1.call-done.shares_ref, bf16[3584,384]{1,0:T(8,128)(2,1)} %constant_dynamic-slice_fusion.x_ref), custom_call_target="tpu_custom_call" | custom-call | tf_op jit(solution)/shard_map/chain/pallas_call | solution.py:156
  428.8 36.3 %all_to_all.19 = bf16[4,896,384]{2,1,0:T(8,128)(2,1)S(1)} all-to-all(bf16[4,896,384]{2,1,0:T(8,128)(2,1)} %bitcast.10), channel_id=1, replica_groups=mesh['row'=4,'col'=8] {'row'}, dimensions={0} | all-to-all | bytes 5505024 | tf_op jit(solution)/shard_map/all_to_all | solution.py:312
  465.2 1.8 copy.5
Async XLA Ops:
  7.2 84.0 %all-gather.3.cloned.1.call-start = ((), (), s32[]{:S(2)}) async-start(), calls=%async_computation.1 | async-start | bytes 13762560 | tf_op jit(solution)/shard_map/all_gather | solution.py:281
  15.1 1.8 copy-start
  15.1 256.2 %all-gather.5.cloned.1.call-start = ((), (), s32[]{:S(2)}) async-start(), calls=%async_computation.2 | async-start | bytes 16558080 | tf_op jit(solution)/shard_map/all_gather | solution.py:303
  96.0 4.0 copy-start.1
Sparse Core Ops, SparseCore 0:
  15.2 75.8 all-gather.2
  162.9 108.4 all-gather.4
where the time goes:
time: 474 us
  Pallas kernels  213 us (45%)
  waiting for transfers between devices  175 us (37%)
  blocking collectives  36.3 us (8%)
  other arithmetic  15.4 us (3%)
  between operations  14.1 us (3%)
  matrix products  12.9 us (3%)
  local copies, waits for them, and re-layouts  7.1 us (1%)
    pallas_call x1, Pallas kernels, chain(): pl.pallas_call(functools.partial(chain_kernel, tile, factor, rows), out_s...  157 us
    all_gather x1, waiting for transfers between devices, per_device(): shares = lax.all_gather(share, ('row', 'col'), axis=0, tiled=True)  105 us
    all_gather x1, waiting for transfers between devices, per_device(): panel = lax.all_gather(base, 'row', axis=0, tiled=True)  70.1 us
    pallas_call x1, Pallas kernels, ring_sum(): pl.pallas_call(ring_kernel, out_shape=jax.ShapeDtypeStruct((height, block...  55.3 us
    all_to_all x1, blocking collectives, per_device(): update = lax.all_to_all(update, 'row', 0, 1, tiled=True)  36.3 us
    dot_general x3, matrix products, outer_rows(): lax.dot_general(left, right, (((1,), (1,)), ((), ())), preferred_element_...  12.9 us
  transfers between devices with their start and end apart: 2, of which 2 were waited for; matrix products, arithmetic and copies ran while one was open for 2% of the time, Pallas kernels for 0%

commit v1 on v0

--- a/solution.py
+++ b/solution.py
@@ -268,6 +268,553 @@
     )(partial_value.reshape(count, height, block))
 
 
+LANES = 128
+
+
+def ring_place(column, count):
+    odd, pair = lax.rem(column, 2), lax.div(column, 2)
+    return (1 - odd) * pair + odd * (count - 1 - pair)
+
+
+def ring_column(spot, count):
+    spot = lax.rem(spot + 2 * count, count)
+    back = lax.div(spot, count // 2)
+    return (1 - back) * 2 * spot + back * (2 * (count - 1 - spot) + 1)
+
+
+def flipped(row, bits):
+    chip, core = lax.div(row, 2), lax.rem(row, 2)
+    if bits & 2:
+        chip = 1 - chip
+    if bits & 1:
+        core = 1 - core
+    return 2 * chip + core
+
+
+def meet(barrier, targets):
+    for target in targets:
+        pl.semaphore_signal(
+            barrier, inc=1, device_id=target, device_id_type=pl.DeviceIdType.MESH
+        )
+    pl.semaphore_wait(barrier, len(targets))
+
+
+def remote(source, target, send_sem, recv_sem, device):
+    return pltpu.make_async_remote_copy(
+        src_ref=source,
+        dst_ref=target,
+        send_sem=send_sem,
+        recv_sem=recv_sem,
+        device_id=device,
+        device_id_type=pl.DeviceIdType.MESH,
+    )
+
+
+def share_kernel(
+    count, wide, base_ref, share_ref, slab_ref, panel, partial, landed, running,
+    panel_send, panel_recv, own_sem, ring_send, ring_recv,
+):
+    chunks = panel.shape[1]
+    block = chunks * LANES
+    strip = block // count
+    width = panel.shape[3] // 4
+    me, column = lax.axis_index("row"), lax.axis_index("col")
+    core = lax.rem(me, 2)
+    place = ring_place(column, count)
+    sign = 1 - 2 * core
+    ways = (sign, -sign)
+    meet(
+        pltpu.get_barrier_semaphore(),
+        [{"col": ring_column(place + way, count)} for way in ways]
+        + [{"row": flipped(me, 1)}, {"row": flipped(me, 2)}],
+    )
+
+    def pass_on(slot, source, chunk):
+        return remote(
+            source,
+            panel.at[slot, chunk],
+            panel_send.at[slot - 1, chunk],
+            panel_recv.at[slot - 1, chunk],
+            {"row": flipped(me, 2 if slot == 2 else 1)},
+        )
+
+    own = pltpu.make_async_copy(base_ref, panel.at[0], own_sem)
+    own.start()
+    for chunk in range(chunks):
+        pass_on(2, base_ref.at[chunk], chunk).start()
+        pass_on(1, base_ref.at[chunk], chunk).start()
+    own.wait()
+
+    @pl.loop(0, 4 * chunks)
+    def _(event):
+        far = event >= 2 * chunks
+        late = lax.max(event - 2 * chunks, 0)
+        slot = jnp.where(far, 2 + lax.rem(late, 2), lax.div(event, chunks))
+        chunk = jnp.where(far, lax.div(late, 2), lax.rem(event, chunks))
+        for x in range(1, 4):
+            @pl.when(slot == x)
+            def _():
+                pass_on(x, panel.at[2 if x == 3 else 0, chunk], chunk).wait_recv()
+                if x == 2:
+                    pass_on(3, panel.at[2, chunk], chunk).start()
+
+        turned = lax.rem(slot, 2)
+        offset = jnp.where(
+            slot == 2, 2, turned * (2 - (1 - 2 * core) * (2 - slot))
+        )
+        owner = lax.rem(me + offset, 4)
+        piece = panel[slot, chunk]
+        target = pl.ds(pl.multiple_of((owner * chunks + chunk) * LANES, LANES), LANES)
+        mine = pl.ds(pl.multiple_of(me * width, LANES), width)
+        slab_ref[:, target] = panel[slot, chunk, :, mine].T
+        spot = offset * chunks + chunk
+
+        @pl.when(spot < chunks + wide - 1)
+        def _():
+            value = outer_rows(panel[0].reshape(block, panel.shape[3]), piece)
+            value = value.astype(jnp.bfloat16)
+            for c in range(count):
+                place_in = spot - c * strip // LANES
+
+                @pl.when((place_in >= 0) & (place_in < wide))
+                def _():
+                    lanes = pl.ds(pl.multiple_of(place_in * LANES, LANES), LANES)
+                    partial[c, :, lanes] = value[c * strip : (c + 1) * strip]
+
+    for slot in range(1, 4):
+        for chunk in range(chunks):
+            pass_on(slot, panel.at[2 if slot == 3 else 0, chunk], chunk).wait_send()
+
+    streams = landed.shape[0]
+    size = landed.shape[3]
+
+    def ring_copy(step, k, source):
+        return remote(
+            source,
+            landed.at[k, step],
+            ring_send.at[k, step],
+            ring_recv.at[k, step],
+            {"col": ring_column(place + ways[k % 2], count)},
+        )
+
+    copies = []
+    for k in range(streams):
+        lanes = pl.ds(k * size, size)
+        source = partial.at[ring_column(place - ways[k % 2], count), :, lanes]
+        copies.append(ring_copy(0, k, source))
+        copies[k].start()
+    sent = list(copies)
+    for step in range(count - 1):
+        for k in range(streams):
+            lanes = pl.ds(k * size, size)
+            copies[k].wait_recv()
+            mine = partial[ring_column(place - ways[k % 2] * (step + 2), count), :, lanes]
+            value = landed[k, step].astype(jnp.float32) + mine.astype(jnp.float32)
+            value = value.astype(jnp.bfloat16)
+            if step < count - 2:
+                running[k, step] = value
+                copies[k] = ring_copy(step + 1, k, running.at[k, step])
+                copies[k].start()
+                sent.append(copies[k])
+            else:
+                share_ref[:, lanes] = value
+    for copy in sent:
+        copy.wait_send()
+
+
+def summed_share(base, count, wide):
+    block, width = base.shape
+    strip = block // count
+    chunks = block // LANES
+    streams = 4
+    piece = wide * LANES // streams
+    vmem = pl.BlockSpec(memory_space=pltpu.VMEM)
+    return pl.pallas_call(
+        functools.partial(share_kernel, count, wide),
+        out_shape=(
+            jax.ShapeDtypeStruct((strip, wide * LANES), jnp.bfloat16),
+            jax.ShapeDtypeStruct((width // 4, 4 * block), jnp.bfloat16),
+        ),
+        in_specs=[pl.BlockSpec(memory_space=pl.ANY)],
+        out_specs=(vmem, vmem),
+        scratch_shapes=[
+            pltpu.VMEM((4, chunks, LANES, width), jnp.bfloat16),
+            pltpu.VMEM((count, strip, wide * LANES), jnp.bfloat16),
+            pltpu.VMEM((streams, count - 1, strip, piece), jnp.bfloat16),
+            pltpu.VMEM((streams, count - 1, strip, piece), jnp.bfloat16),
+            pltpu.SemaphoreType.DMA((3, chunks)),
+            pltpu.SemaphoreType.DMA((3, chunks)),
+            pltpu.SemaphoreType.DMA,
+            pltpu.SemaphoreType.DMA((streams, count - 1)),
+            pltpu.SemaphoreType.DMA((streams, count - 1)),
+        ],
+        compiler_params=pltpu.CompilerParams(
+            collective_id=1, has_side_effects=True, vmem_limit_bytes=48 * 1024 * 1024
+        ),
+        name="summed_share",
+    )(base.reshape(chunks, LANES, width))
+
+
+def gather_plan(count):
+    hops = (count // 2, count - 1 - count // 2)
+    ring = [(w, s) for s in range(1, hops[0] + 1) for w in (0, 1) if s <= hops[w]]
+    order = []
+    first = [("a",) + hop for hop in ring]
+    second = [("b", x) + hop for hop in ring for x in (0, 1)]
+    second.sort(key=lambda m: (m[3], m[1], m[2]))
+    third = [("ya", 0, 0)] + [("ya",) + hop for hop in ring]
+    order += [first[0], first[1], ("start_b",), ("yb",), third[0]]
+    order += [first[2], first[3], third[1]]
+    rest = first[4:]
+    tail = []
+    index = 2
+    while second or rest:
+        for source, amount in ((rest, 2), (second, 2)):
+            for _ in range(amount):
+                if source:
+                    tail.append(source.pop(0))
+        if index < len(third):
+            tail.append(third[index])
+            index += 1
+    tail += third[index:]
+    return hops, order + tail
+
+
+def gather_names(count):
+    _, order = gather_plan(count)
+    arrivals = [m for m in order if m[0] != "start_b"]
+    partner = [("p",) + m for m in arrivals] + [("p", "own_a"), ("p", "own_b")]
+    return {name: number for number, name in enumerate(arrivals + partner)}
+
+
+def gather_steps(count, head, land, send_sems, recv_sems):
+    me, column = lax.axis_index("row"), lax.axis_index("col")
+    place = ring_place(column, count)
+    sign = 1 - 2 * lax.rem(me, 2)
+    ways = (sign, -sign)
+    (long, short), order = gather_plan(count)
+    hops = (long, short)
+    names = gather_names(count)
+    strip = land.shape[1]
+    rows = {"a": pl.ds(0, head), "b": pl.ds(head, strip - head)}
+
+    def where(name, mirrored=False):
+        kind = name[0]
+        if kind == "p":
+            return where(name[1:], True)
+        w, s, bits, part = 0, 0, 0, kind[-1]
+        if kind in ("a", "ya"):
+            w, s = name[1], name[2]
+            bits = 2 if kind == "ya" else 0
+        elif kind == "b":
+            bits, w, s = 2 * name[1], name[2], name[3]
+        elif kind == "yb":
+            bits = 2
+        if mirrored:
+            bits = bits + 1
+        way = -ways[w] if mirrored else ways[w]
+        owner = flipped(me, bits) * count + ring_column(place - way * s, count)
+        return land.at[owner, rows[part]]
+
+    def target(name):
+        if name[0] == "p":
+            return {"row": flipped(me, 1)}
+        if name[0] in ("ya", "yb"):
+            return {"row": flipped(me, 2)}
+        w = name[1] if name[0] == "a" else name[2]
+        return {"col": ring_column(place + ways[w], count)}
+
+    def copy_of(name, source):
+        number = names[name]
+        return remote(source, source, send_sems.at[number], recv_sems.at[number], target(name))
+
+    sent = []
+
+    def send(name, held):
+        copy = copy_of(name, held)
+        copy.start()
+        sent.append(copy)
+
+    own_a, own_b = where(("own_a",)), where(("own_b",))
+
+    def begin():
+        send(("a", 0, 1), own_a)
+        send(("a", 1, 1), own_a)
+        send(("yb",), own_b)
+        send(("ya", 0, 0), own_a)
+        send(("p", "own_a"), own_a)
+        send(("p", "own_b"), own_b)
+
+    def arrive(name):
+        held = where(name)
+        copy_of(name, held).wait_recv()
+        if name[0] == "a":
+            w, s = name[1:]
+            if s < hops[w]:
+                send(("a", w, s + 1), held)
+            send(("ya", w, s), held)
+        elif name[0] == "b":
+            x, w, s = name[1:]
+            if s < hops[w]:
+                send(("b", x, w, s + 1), held)
+        elif name[0] == "yb":
+            send(("b", 1, 0, 1), held)
+            send(("b", 1, 1, 1), held)
+        send(("p",) + name, held)
+
+    def step_of(name):
+        if name[0] == "start_b":
+            def start_b():
+                send(("b", 0, 0, 1), own_b)
+                send(("b", 0, 1, 1), own_b)
+
+            return start_b
+        return functools.partial(arrive, name)
+
+    def finish():
+        for name in names:
+            if name[0] == "p":
+                held = where(name)
+                copy_of(name, held).wait_recv()
+        for name in names:
+            copy_of(name, own_a if rows_of(name) == "a" else own_b).wait_send()
+
+    def rows_of(name):
+        kind = name[1] if name[0] == "p" else name[0]
+        return kind[-1]
+
+    return begin, [step_of(name) for name in order], finish
+
+
+def update_kernel(
+    count, factor, head, share_ref, slab_ref, out_ref, gram, land, first, rough, exact,
+    stage, sends, recvs, own_sem, free_sem, out_send, out_recv,
+):
+    size = gram.shape[0]
+    blocks = size // LANES
+    strip, reach = land.shape[1:]
+    wide = reach // LANES
+    width = slab_ref.shape[0]
+    tile = 512 if size % 512 == 0 else LANES
+    block = size // 4
+    me, column = lax.axis_index("row"), lax.axis_index("col")
+    place = ring_place(column, count)
+    number = me * count + column
+    ring = [{"col": ring_column(place + way, count)} for way in (1, -1)]
+    near = ring + [{"row": flipped(me, bits)} for bits in (1, 2)]
+    meet(pltpu.get_barrier_semaphore(), near + [{"row": flipped(me, 3)}])
+
+    def begin_of(strip_number):
+        return lax.div(strip_number * strip, LANES)
+
+    def column_block(index):
+        return pl.ds(pl.multiple_of(lax.rem(index, blocks) * LANES, LANES), LANES)
+
+    def row_strip(strip_number):
+        return pl.ds(pl.multiple_of(strip_number * strip, 16), strip)
+
+    def assemble():
+        @pl.loop(0, land.shape[0])
+        def _(k):
+            base = begin_of(k)
+            for t in range(wide):
+                gram[row_strip(k), column_block(base + t)] = land[
+                    k, :, t * LANES : (t + 1) * LANES
+                ]
+
+        def body(i, carry):
+            single, double = carry
+            here = column_block(i)
+
+            def squares(total, piece):
+                value = piece.astype(jnp.float32)
+                return total + jnp.sum(value * value, axis=0, keepdims=True)
+
+            single = squares(single, gram[here, here])
+            for d in range(1, blocks // 2):
+                there = column_block(i + d)
+                piece = gram[here, there]
+                gram[there, here] = piece.T
+                double = squares(double, piece)
+            single = squares(single, gram[here, column_block(i + blocks // 2)])
+            return single, double
+
+        zero = jnp.zeros((1, LANES), jnp.float32)
+        single, double = lax.fori_loop(0, blocks, body, (zero, zero))
+        return jnp.sum(single + 2.0 * double, axis=1, keepdims=True)
+
+    own = pltpu.make_async_copy(share_ref, land.at[number], own_sem)
+    own.start()
+    own.wait()
+    begin, steps, finish = gather_steps(count, head, land, sends.at[0], recvs.at[0])
+    begin()
+    for step in steps:
+        step()
+    finish()
+    quartic = assemble()
+    for target in near:
+        pl.semaphore_signal(
+            free_sem, inc=1, device_id=target, device_id_type=pl.DeviceIdType.MESH
+        )
+    scale = 1.0 / jnp.sqrt(jnp.sqrt(quartic) + EPSILON)
+    square = scale * scale
+
+    def times_gram(source, finish, hooks=()):
+        @pl.loop(0, size // tile)
+        def _(step):
+            for k, calls in enumerate(hooks):
+                if calls:
+                    @pl.when(step == k)
+                    def _():
+                        for call in calls:
+                            call()
+
+            columns = pl.ds(pl.multiple_of(step * tile, tile), tile)
+            finish(
+                columns,
+                jnp.dot(source[...], gram[:, columns], preferred_element_type=jnp.float32),
+            )
+
+    part = exact.at[pl.ds(0, strip)]
+    left, right = rough.at[pl.ds(0, strip)], first.at[pl.ds(0, strip)]
+    mine = gram.at[row_strip(number)]
+
+    def after_square(columns, value):
+        value = value * square * square
+        part[:, columns] = (
+            COEF_LINEAR * (mine[:, columns].astype(jnp.float32) * square)
+            + COEF_CUBIC * value
+        )
+        left[:, columns] = value.astype(jnp.bfloat16)
+
+    def after_cube(columns, value):
+        right[:, columns] = (
+            part[:, columns] + COEF_QUINTIC * (value * square)
+        ).astype(jnp.bfloat16)
+
+    def after_third(columns, value):
+        value = value * square
+        part[:, columns] = (
+            COEF_LINEAR * right[:, columns].astype(jnp.float32) + COEF_CUBIC * value
+        )
+        left[:, columns] = value.astype(jnp.bfloat16)
+
+    def after_fourth(columns, value):
+        right[:, columns] = (
+            part[:, columns] + COEF_QUINTIC * (value * square)
+        ).astype(jnp.bfloat16)
+
+    times_gram(mine, after_square)
+    times_gram(left, after_cube)
+    times_gram(right, after_third)
+    times_gram(left, after_fourth)
+
+    pl.semaphore_wait(free_sem, len(near))
+    base = begin_of(number)
+    for t in range(wide):
+        land[number, :, t * LANES : (t + 1) * LANES] = right[:, column_block(base + t)]
+
+    begin, steps, finish = gather_steps(count, head, land, sends.at[1], recvs.at[1])
+    begin()
+    slots = size // tile
+    paced = [[] for _ in range(2 * slots)]
+    for k, step in enumerate(steps):
+        paced[min(2 * slots - 1, k * 5 // 6)].append(step) if k * 5 // 6 < 2 * slots else None
+    early = sum(len(calls) for calls in paced)
+
+    def keep(columns, value):
+        value = value * square
+        exact[:, columns] = (
+            COEF_LINEAR * slab_ref[:, columns].astype(jnp.float32) + COEF_CUBIC * value
+        )
+        rough[:, columns] = value.astype(jnp.bfloat16)
+
+    def combine(columns, value):
+        first[:, columns] = (
+            exact[:, columns] + COEF_QUINTIC * (value * square)
+        ).astype(jnp.bfloat16)
+
+    times_gram(slab_ref, keep, paced[:slots])
+    times_gram(rough, combine, paced[slots:])
+    for step in steps[early:]:
+        step()
+    finish()
+    assemble()
+
+    def after_product(columns, value):
+        exact[:, columns] = (
+            COEF_LINEAR * first[:, columns].astype(jnp.float32) + COEF_CUBIC * value
+        )
+        rough[:, columns] = value.astype(jnp.bfloat16)
+
+    times_gram(first, after_product)
+
+    lanes = pl.ds(pl.multiple_of(me * width, LANES), width)
+
+    def out_copy(bits):
+        return remote(
+            stage.at[bits],
+            out_ref.at[:, lanes],
+            out_send.at[bits - 1],
+            out_recv.at[bits - 1],
+            {"row": flipped(me, bits)},
+        )
+
+    @pl.loop(0, 4)
+    def _(step):
+        bits = 3 - step
+        chip, core = lax.div(me, 2), lax.rem(me, 2)
+        high, low = lax.div(bits, 2), lax.rem(bits, 2)
+        owner = 2 * (chip + high - 2 * chip * high) + (core + low - 2 * core * low)
+        columns = pl.ds(pl.multiple_of(owner * block, LANES), block)
+        value = jnp.dot(rough[...], gram[:, columns], preferred_element_type=jnp.float32)
+        value = (exact[:, columns] + COEF_QUINTIC * value) * (scale * factor)
+        stage[bits] = value.astype(jnp.bfloat16).T
+        for x in range(1, 4):
+            @pl.when(bits == x)
+            def _():
+                out_copy(x).start()
+
+    kept = pltpu.make_async_copy(stage.at[0], out_ref.at[:, lanes], own_sem)
+    kept.start()
+    kept.wait()
+    for bits in range(1, 4):
+        out_copy(bits).wait()
+
+
+def updated(share, slab, factor, count, wide):
+    width, size = slab.shape
+    strip = share.shape[0]
+    head = strip * 4 // 7 // 16 * 16
+    vmem = pl.BlockSpec(memory_space=pltpu.VMEM)
+    half = pltpu.VMEM((width, size), jnp.bfloat16)
+    messages = len(gather_names(count))
+    return pl.pallas_call(
+        functools.partial(update_kernel, count, factor, head),
+        out_shape=jax.ShapeDtypeStruct((size // 4, 4 * width), jnp.bfloat16),
+        in_specs=[vmem, vmem],
+        out_specs=pl.BlockSpec(memory_space=pl.ANY),
+        scratch_shapes=[
+            pltpu.VMEM((size, size), jnp.bfloat16),
+            pltpu.VMEM((4 * count, strip, wide * LANES), jnp.bfloat16),
+            half,
+            half,
+            pltpu.VMEM((width, size), jnp.float32),
+            pltpu.VMEM((4, size // 4, width), jnp.bfloat16),
+            pltpu.SemaphoreType.DMA((2, messages)),
+            pltpu.SemaphoreType.DMA((2, messages)),
+            pltpu.SemaphoreType.DMA,
+            pltpu.SemaphoreType.REGULAR,
+            pltpu.SemaphoreType.DMA((3,)),
+            pltpu.SemaphoreType.DMA((3,)),
+        ],
+        compiler_params=pltpu.CompilerParams(
+            collective_id=2, has_side_effects=True, vmem_limit_bytes=63 * 1024 * 1024
+        ),
+        name="updated",
+    )(share, slab)
+
+
 def per_device(factor, gradient, momentum):
     rows = lax.axis_size("row")
     grad32 = gradient.astype(jnp.float32)
@@ -275,6 +822,21 @@
     nesterov = grad32 + MOMENTUM_DECAY * buffer
     base = nesterov.astype(jnp.bfloat16)
     block = base.shape[0]
+    count = lax.axis_size("col")
+    strip = block // count
+    if (
+        rows == 4
+        and count % 2 == 0
+        and count >= 4
+        and block % LANES == 0
+        and base.shape[1] % (4 * LANES) == 0
+        and strip * count == block
+        and strip % 16 == 0
+        and 32 <= strip <= LANES
+    ):
+        wide = 4 * block // LANES // 2 + 2
+        share, slab = summed_share(base, count, wide)
+        return (updated(share, slab, factor, count, wide), buffer)
     half = block // 2
     middle = rows // 2
     me = lax.axis_index("row")

time: 474 us -> 364 us (0.77)
  waiting for transfers between devices: 175 us -> 0 us
  Pallas kernels: 213 us -> 350 us
  blocking collectives: 36.3 us -> 0 us
  between operations: 14.1 us -> 0.65 us
  matrix products: 12.9 us -> 0 us
  other arithmetic: 15.4 us -> 6.99 us
    all_gather x2 -> x0, waiting for transfers between devices: 175 us -> none  [the longest x1 105 us: per_device(): shares = lax.all_gather(share, ('row', 'col'), axis=0, tiled=True)]
    pallas_call x2, Pallas kernels: 213 us -> 350 us  [the longest x1 246 us: updated(): pl.pallas_call(functools.partial(update_kernel, count, factor, head), out...]
    all_to_all x1 -> x0, blocking collectives: 36.3 us -> none  [per_device(): update = lax.all_to_all(update, 'row', 0, 1, tiled=True)]
    dot_general x3 -> x0, matrix products: 12.9 us -> none  [outer_rows(): lax.dot_general(left, right, (((1,), (1,)), ((), ())), preferred_element_...]
    concatenate x1 -> x0, other arithmetic: 7.55 us -> none  [per_device(): jnp.concatenate([part.astype(jnp.bfloat16) for part in parts], axis=0)]
  transfers between devices with their start and end apart: 2 -> 0, of which waited for: 2 -> 0; matrix products, arithmetic and copies ran while one was open for 2% -> 0% of each run, Pallas kernels for 0% -> 0%
where the time goes in v1:
time: 364 us
  Pallas kernels  350 us (96%)
  other arithmetic  6.99 us (2%)
  local copies, waits for them, and re-layouts  5.8 us (2%)
    pallas_call x1, Pallas kernels, updated(): pl.pallas_call(functools.partial(update_kernel, count, factor, head), out...  246 us
    pallas_call x1, Pallas kernels, summed_share(): pl.pallas_call(functools.partial(share_kernel, count, wide), out_shape=(j...  104 us

profile of v1, /device:TPU:0, one launch (start us, length us, event | category | flops | bytes accessed | tf_op | source)
XLA Modules:
  0.0 363.9 jit_solution(7981329250843586986)
XLA Ops:
  0.6 7.0 %fusion = (bf16[896,1536]{1,0:T(8,128)(2,1)S(1)}, f32[896,1536]{1,0:T(8,128)}) fusion(bf16[896,1536]{1,0:T(8,128)(2,1)} %param.2, f32[896,1536]{1,0:T(8,128)} %param.3), kind=kLoop, calls=%fused_computation.2 | loop fusion | flops 8257536 | bytes 16515072 | tf_op jit(solution)/shard_map/convert_element_type | solution.py:823
  7.6 104.4 %summed_share.1 = (bf16[112,2048]{1,0:T(8,128)(2,1)S(1)}, bf16[384,3584]{1,0:T(8,128)(2,1)S(1)}) custom-call(bf16[7,128,1536]{2,1,0:T(8,128)(2,1)S(1)} %bitcast.1), custom_call_target="tpu_custom_call" | custom-call | tf_op jit(solution)/shard_map/summed_share/pallas_call | solution.py:432
  112.1 0.0 copy-start
  112.1 1.5 copy-done
  113.6 0.0 copy-start.1
  113.6 0.8 copy-done.1
  114.4 246.0 %updated.1 = bf16[896,1536]{1,0:T(8,128)(2,1)} custom-call(bf16[112,2048]{1,0:T(8,128)(2,1)} %copy-done.1, bf16[384,3584]{1,0:T(8,128)(2,1)} %copy-done), custom_call_target="tpu_custom_call" | custom-call | tf_op jit(solution)/shard_map/updated/pallas_call | solution.py:792
  360.4 3.5 copy.5
Async XLA Ops:
  112.1 1.5 copy-start
  113.6 0.8 copy-start.1

commit v2 on v1

--- a/solution.py
+++ b/solution.py
@@ -373,51 +373,58 @@
         def _():
             value = outer_rows(panel[0].reshape(block, panel.shape[3]), piece)
             value = value.astype(jnp.bfloat16)
-            for c in range(count):
-                place_in = spot - c * strip // LANES
+            for i in range(chunks):
+                place_in = spot - i
 
                 @pl.when((place_in >= 0) & (place_in < wide))
                 def _():
                     lanes = pl.ds(pl.multiple_of(place_in * LANES, LANES), LANES)
-                    partial[c, :, lanes] = value[c * strip : (c + 1) * strip]
+                    held = slice(i * LANES, (i + 1) * LANES)
+                    partial[held, lanes] = value[held]
 
     for slot in range(1, 4):
         for chunk in range(chunks):
             pass_on(slot, panel.at[2 if slot == 3 else 0, chunk], chunk).wait_send()
 
-    streams = landed.shape[0]
     size = landed.shape[3]
+    lanes = [
+        pl.ds(start, min(size, wide * LANES - start))
+        for start in range(0, wide * LANES, size)
+    ]
+
+    def strip_at(spot):
+        spot = lax.rem(spot + 2 * count, count)
+        return pl.ds(pl.multiple_of(spot * strip, 16), strip)
 
     def ring_copy(step, k, source):
         return remote(
             source,
-            landed.at[k, step],
+            landed.at[k, step, :, pl.ds(0, lanes[k].size)],
             ring_send.at[k, step],
             ring_recv.at[k, step],
             {"col": ring_column(place + ways[k % 2], count)},
         )
 
     copies = []
-    for k in range(streams):
-        lanes = pl.ds(k * size, size)
-        source = partial.at[ring_column(place - ways[k % 2], count), :, lanes]
+    for k in range(len(lanes)):
+        source = partial.at[strip_at(place - ways[k % 2]), lanes[k]]
         copies.append(ring_copy(0, k, source))
         copies[k].start()
     sent = list(copies)
     for step in range(count - 1):
-        for k in range(streams):
-            lanes = pl.ds(k * size, size)
+        for k in range(len(lanes)):
+            held = pl.ds(0, lanes[k].size)
             copies[k].wait_recv()
-            mine = partial[ring_column(place - ways[k % 2] * (step + 2), count), :, lanes]
-            value = landed[k, step].astype(jnp.float32) + mine.astype(jnp.float32)
+            mine = partial[strip_at(place - ways[k % 2] * (step + 2)), lanes[k]]
+            value = landed[k, step, :, held].astype(jnp.float32) + mine.astype(jnp.float32)
             value = value.astype(jnp.bfloat16)
             if step < count - 2:
-                running[k, step] = value
-                copies[k] = ring_copy(step + 1, k, running.at[k, step])
+                running[k, step, :, held] = value
+                copies[k] = ring_copy(step + 1, k, running.at[k, step, :, held])
                 copies[k].start()
                 sent.append(copies[k])
             else:
-                share_ref[:, lanes] = value
+                share_ref[:, lanes[k]] = value
     for copy in sent:
         copy.wait_send()
 
@@ -427,7 +434,7 @@
     strip = block // count
     chunks = block // LANES
     streams = 4
-    piece = wide * LANES // streams
+    piece = pl.cdiv(wide, streams) * LANES
     vmem = pl.BlockSpec(memory_space=pltpu.VMEM)
     return pl.pallas_call(
         functools.partial(share_kernel, count, wide),
@@ -439,7 +446,7 @@
         out_specs=(vmem, vmem),
         scratch_shapes=[
             pltpu.VMEM((4, chunks, LANES, width), jnp.bfloat16),
-            pltpu.VMEM((count, strip, wide * LANES), jnp.bfloat16),
+            pltpu.VMEM((block, wide * LANES), jnp.bfloat16),
             pltpu.VMEM((streams, count - 1, strip, piece), jnp.bfloat16),
             pltpu.VMEM((streams, count - 1, strip, piece), jnp.bfloat16),
             pltpu.SemaphoreType.DMA((3, chunks)),
@@ -458,26 +465,21 @@
 def gather_plan(count):
     hops = (count // 2, count - 1 - count // 2)
     ring = [(w, s) for s in range(1, hops[0] + 1) for w in (0, 1) if s <= hops[w]]
-    order = []
     first = [("a",) + hop for hop in ring]
     second = [("b", x) + hop for hop in ring for x in (0, 1)]
     second.sort(key=lambda m: (m[3], m[1], m[2]))
     third = [("ya", 0, 0)] + [("ya",) + hop for hop in ring]
-    order += [first[0], first[1], ("start_b",), ("yb",), third[0]]
+    order = [first[0], first[1], ("start_b",), ("yb",), third[0]]
     order += [first[2], first[3], third[1]]
     rest = first[4:]
-    tail = []
     index = 2
     while second or rest:
-        for source, amount in ((rest, 2), (second, 2)):
-            for _ in range(amount):
-                if source:
-                    tail.append(source.pop(0))
-        if index < len(third):
-            tail.append(third[index])
-            index += 1
-    tail += third[index:]
-    return hops, order + tail
+        for source in (rest, second):
+            order += source[:2]
+            del source[:2]
+        order += third[index : index + 1]
+        index += 1
+    return hops, order + third[index:]
 
 
 def gather_names(count):
@@ -487,16 +489,49 @@
     return {name: number for number, name in enumerate(arrivals + partner)}
 
 
-def gather_steps(count, head, land, send_sems, recv_sems):
+def strip_names(bits, u):
+    if u == 0:
+        near = [[], [("ya", 0, 0), ("yb",)]][bits // 2]
+        if bits == 1:
+            return [("p", "own_a"), ("p", "own_b")]
+    else:
+        w, s = (0, -u) if u < 0 else (1, u)
+        near = [("ya" if bits & 2 else "a", w, s), ("b", bits // 2, w, s)]
+    return [("p",) + m for m in near] if bits & 1 else near
+
+
+def gather_groups(count, width):
+    (long, short), order = gather_plan(count)
+    works = []
+    for bits in range(4):
+        for u in range(-long, short + 1):
+            after = u + 1 if u < short else -long
+            works.append((bits, u, strip_names(bits, u) + strip_names(bits, after)))
+    seen = set()
+    groups = []
+    for start in range(0, len(order), width):
+        events = order[start : start + width]
+        due = set(seen)
+        seen.update(events)
+        ready = []
+        for work in list(works):
+            names = [m[1:] if m[0] == "p" else m for m in work[2]]
+            known = due if work[0] & 1 else seen
+            if all(m in known or m[0] in ("own_a", "own_b") for m in names):
+                works.remove(work)
+                ready.append(work)
+        groups.append((events, ready))
+    groups.append(([], works))
+    return groups
+
+
+def gather_steps(count, head, strip, land, send_sems, recv_sems):
     me, column = lax.axis_index("row"), lax.axis_index("col")
     place = ring_place(column, count)
     sign = 1 - 2 * lax.rem(me, 2)
     ways = (sign, -sign)
-    (long, short), order = gather_plan(count)
-    hops = (long, short)
+    hops, _ = gather_plan(count)
     names = gather_names(count)
-    strip = land.shape[1]
-    rows = {"a": pl.ds(0, head), "b": pl.ds(head, strip - head)}
 
     def where(name, mirrored=False):
         kind = name[0]
@@ -513,8 +548,11 @@
         if mirrored:
             bits = bits + 1
         way = -ways[w] if mirrored else ways[w]
-        owner = flipped(me, bits) * count + ring_column(place - way * s, count)
-        return land.at[owner, rows[part]]
+        spot = lax.rem(place - way * s + count, count)
+        start = (flipped(me, bits) * count + spot) * strip
+        if part == "b":
+            return land.at[pl.ds(pl.multiple_of(start + head, 16), strip - head)]
+        return land.at[pl.ds(pl.multiple_of(start, 16), head)]
 
     def target(name):
         if name[0] == "p":
@@ -528,12 +566,8 @@
         number = names[name]
         return remote(source, source, send_sems.at[number], recv_sems.at[number], target(name))
 
-    sent = []
-
     def send(name, held):
-        copy = copy_of(name, held)
-        copy.start()
-        sent.append(copy)
+        copy_of(name, held).start()
 
     own_a, own_b = where(("own_a",)), where(("own_b",))
 
@@ -546,6 +580,10 @@
         send(("p", "own_b"), own_b)
 
     def arrive(name):
+        if name[0] == "start_b":
+            send(("b", 0, 0, 1), own_b)
+            send(("b", 0, 1, 1), own_b)
+            return
         held = where(name)
         copy_of(name, held).wait_recv()
         if name[0] == "a":
@@ -562,100 +600,109 @@
             send(("b", 1, 1, 1), held)
         send(("p",) + name, held)
 
-    def step_of(name):
-        if name[0] == "start_b":
-            def start_b():
-                send(("b", 0, 0, 1), own_b)
-                send(("b", 0, 1, 1), own_b)
-
-            return start_b
-        return functools.partial(arrive, name)
-
-    def finish():
+    def land_from_partner(name):
+        copy_of(name, where(name)).wait_recv()
+
+    def sent():
         for name in names:
-            if name[0] == "p":
-                held = where(name)
-                copy_of(name, held).wait_recv()
-        for name in names:
-            copy_of(name, own_a if rows_of(name) == "a" else own_b).wait_send()
-
-    def rows_of(name):
-        kind = name[1] if name[0] == "p" else name[0]
-        return kind[-1]
-
-    return begin, [step_of(name) for name in order], finish
+            kind = name[1] if name[0] == "p" else name[0]
+            copy_of(name, own_a if kind[-1] == "a" else own_b).wait_send()
+
+    return begin, arrive, land_from_partner, sent
 
 
 def update_kernel(
     count, factor, head, share_ref, slab_ref, out_ref, gram, land, first, rough, exact,
-    stage, sends, recvs, own_sem, free_sem, out_send, out_recv,
+    stage, total, sends, recvs, own_sem, free_sem, out_send, out_recv,
 ):
     size = gram.shape[0]
     blocks = size // LANES
-    strip, reach = land.shape[1:]
+    strip, reach = share_ref.shape
     wide = reach // LANES
     width = slab_ref.shape[0]
     tile = 512 if size % 512 == 0 else LANES
     block = size // 4
+    chunks = block // LANES
     me, column = lax.axis_index("row"), lax.axis_index("col")
     place = ring_place(column, count)
-    number = me * count + column
+    sign = 1 - 2 * lax.rem(me, 2)
+    number = me * count + place
     ring = [{"col": ring_column(place + way, count)} for way in (1, -1)]
     near = ring + [{"row": flipped(me, bits)} for bits in (1, 2)]
     meet(pltpu.get_barrier_semaphore(), near + [{"row": flipped(me, 3)}])
 
-    def begin_of(strip_number):
-        return lax.div(strip_number * strip, LANES)
-
     def column_block(index):
         return pl.ds(pl.multiple_of(lax.rem(index, blocks) * LANES, LANES), LANES)
 
-    def row_strip(strip_number):
-        return pl.ds(pl.multiple_of(strip_number * strip, 16), strip)
-
-    def assemble():
-        @pl.loop(0, land.shape[0])
-        def _(k):
-            base = begin_of(k)
-            for t in range(wide):
-                gram[row_strip(k), column_block(base + t)] = land[
-                    k, :, t * LANES : (t + 1) * LANES
-                ]
-
-        def body(i, carry):
-            single, double = carry
-            here = column_block(i)
-
-            def squares(total, piece):
+    mine_rows = pl.ds(pl.multiple_of(number * strip, 16), strip)
+
+    def place_block(i, squares):
+        here = column_block(i)
+        single = double = jnp.zeros((8, LANES), jnp.float32)
+        for d in range(wide):
+            piece = land[here, d * LANES : (d + 1) * LANES]
+            there = column_block(i + d)
+            gram[here, there] = piece
+            if 0 < d < wide - 1:
+                gram[there, here] = piece.T
+            if squares:
                 value = piece.astype(jnp.float32)
-                return total + jnp.sum(value * value, axis=0, keepdims=True)
-
-            single = squares(single, gram[here, here])
-            for d in range(1, blocks // 2):
-                there = column_block(i + d)
-                piece = gram[here, there]
-                gram[there, here] = piece.T
-                double = squares(double, piece)
-            single = squares(single, gram[here, column_block(i + blocks // 2)])
-            return single, double
-
-        zero = jnp.zeros((1, LANES), jnp.float32)
-        single, double = lax.fori_loop(0, blocks, body, (zero, zero))
-        return jnp.sum(single + 2.0 * double, axis=1, keepdims=True)
-
-    own = pltpu.make_async_copy(share_ref, land.at[number], own_sem)
+                value = jnp.sum((value * value).reshape(LANES // 8, 8, LANES), axis=0)
+                if 0 < d < wide - 1:
+                    double = double + value
+                else:
+                    single = single + value
+        if squares:
+            total[...] += single + 2.0 * double
+
+    def place_blocks(works, squares):
+        if not works:
+            return
+
+        @pl.loop(0, len(works))
+        def _(step):
+            bits, u = works[0][:2]
+            code = jnp.int32(bits * 2 * count + u + count)
+            for k, (bits, u, _) in enumerate(works[1:], 1):
+                code = jnp.where(step == k, bits * 2 * count + u + count, code)
+            bits, u = lax.div(code, 2 * count), lax.rem(code, 2 * count) - count
+            high, low = lax.div(bits, 2), lax.rem(bits, 2)
+            chip, core = lax.div(me, 2), lax.rem(me, 2)
+            row = 2 * (chip + high - 2 * chip * high) + (core + low - 2 * core * low)
+            way = sign * (1 - 2 * low)
+            spot = lax.rem(place + way * u + lax.div(way - 1, 2) + 2 * count, count)
+
+            @pl.when(spot < chunks)
+            def _():
+                place_block(row * chunks + spot, squares)
+
+    own = pltpu.make_async_copy(share_ref, land.at[mine_rows], own_sem)
     own.start()
     own.wait()
-    begin, steps, finish = gather_steps(count, head, land, sends.at[0], recvs.at[0])
-    begin()
-    for step in steps:
-        step()
-    finish()
-    quartic = assemble()
+    total[...] = jnp.zeros_like(total)
+
+    def run_groups(groups, steps, squares):
+        _, arrive, land_from_partner, sent = steps
+        waited = set()
+        for events, works in groups:
+            for name in events:
+                arrive(name)
+            for _, _, names in works:
+                for name in names:
+                    if name[0] == "p" and name not in waited:
+                        waited.add(name)
+                        land_from_partner(name)
+            place_blocks(works, squares)
+        sent()
+
+    steps = gather_steps(count, head, strip, land, sends.at[0], recvs.at[0])
+    steps[0]()
+    run_groups(gather_groups(count, 4), steps, True)
     for target in near:
         pl.semaphore_signal(
             free_sem, inc=1, device_id=target, device_id_type=pl.DeviceIdType.MESH
         )
+    quartic = jnp.sum(jnp.sum(total[...], axis=0, keepdims=True), axis=1, keepdims=True)
     scale = 1.0 / jnp.sqrt(jnp.sqrt(quartic) + EPSILON)
     square = scale * scale
 
@@ -677,7 +724,7 @@
 
     part = exact.at[pl.ds(0, strip)]
     left, right = rough.at[pl.ds(0, strip)], first.at[pl.ds(0, strip)]
-    mine = gram.at[row_strip(number)]
+    mine = gram.at[mine_rows]
 
     def after_square(columns, value):
         value = value * square * square
@@ -699,28 +746,39 @@
         )
         left[:, columns] = value.astype(jnp.bfloat16)
 
-    def after_fourth(columns, value):
-        right[:, columns] = (
-            part[:, columns] + COEF_QUINTIC * (value * square)
-        ).astype(jnp.bfloat16)
-
     times_gram(mine, after_square)
     times_gram(left, after_cube)
     times_gram(right, after_third)
-    times_gram(left, after_fourth)
+    times_gram(left, after_cube)
 
     pl.semaphore_wait(free_sem, len(near))
-    base = begin_of(number)
-    for t in range(wide):
-        land[number, :, t * LANES : (t + 1) * LANES] = right[:, column_block(base + t)]
-
-    begin, steps, finish = gather_steps(count, head, land, sends.at[1], recvs.at[1])
-    begin()
+    for group in range(strip // 16):
+        sixteenth = number * (strip // 16) + group
+        base = lax.div(sixteenth, LANES // 16)
+        rows = pl.ds(pl.multiple_of(sixteenth * 16, 16), 16)
+        for t in range(wide):
+            land[rows, t * LANES : (t + 1) * LANES] = right[
+                group * 16 : group * 16 + 16, column_block(base + t)
+            ]
+
+    steps = gather_steps(count, head, strip, land, sends.at[1], recvs.at[1])
+    steps[0]()
+    groups = gather_groups(count, 4)
     slots = size // tile
     paced = [[] for _ in range(2 * slots)]
-    for k, step in enumerate(steps):
-        paced[min(2 * slots - 1, k * 5 // 6)].append(step) if k * 5 // 6 < 2 * slots else None
-    early = sum(len(calls) for calls in paced)
+    early, waiting = [], []
+    for k, (events, works) in enumerate(groups):
+        if len(early) + len(events) <= 18:
+            early += events
+            waiting += works
+            groups[k] = ([], [])
+        else:
+            groups[k] = (events, waiting + works)
+            break
+    for k, name in enumerate(early):
+        paced[min(2 * slots - 1, k * 2 * slots // len(early))].append(
+            functools.partial(steps[1], name)
+        )
 
     def keep(columns, value):
         value = value * square
@@ -736,10 +794,7 @@
 
     times_gram(slab_ref, keep, paced[:slots])
     times_gram(rough, combine, paced[slots:])
-    for step in steps[early:]:
-        step()
-    finish()
-    assemble()
+    run_groups(groups, steps, False)
 
     def after_product(columns, value):
         exact[:, columns] = (
@@ -796,11 +851,12 @@
         out_specs=pl.BlockSpec(memory_space=pl.ANY),
         scratch_shapes=[
             pltpu.VMEM((size, size), jnp.bfloat16),
-            pltpu.VMEM((4 * count, strip, wide * LANES), jnp.bfloat16),
+            pltpu.VMEM((size, wide * LANES), jnp.bfloat16),
             half,
             half,
             pltpu.VMEM((width, size), jnp.float32),
             pltpu.VMEM((4, size // 4, width), jnp.bfloat16),
+            pltpu.VMEM((8, LANES), jnp.float32),
             pltpu.SemaphoreType.DMA((2, messages)),
             pltpu.SemaphoreType.DMA((2, messages)),
             pltpu.SemaphoreType.DMA,
@@ -832,9 +888,10 @@
         and base.shape[1] % (4 * LANES) == 0
         and strip * count == block
         and strip % 16 == 0
-        and 32 <= strip <= LANES
+        and 32 <= strip < LANES
+        and block // LANES + 1 == count
     ):
-        wide = 4 * block // LANES // 2 + 2
+        wide = 4 * block // LANES // 2 + 1
         share, slab = summed_share(base, count, wide)
         return (updated(share, slab, factor, count, wide), buffer)
     half = block // 2

time: 364 us -> 299 us (0.82)
  Pallas kernels: 350 us -> 285 us
    pallas_call x1, Pallas kernels: 246 us -> 182 us  [updated(): pl.pallas_call(functools.partial(update_kernel, count, factor, head), out...]
where the time goes in v2:
time: 299 us; the launch traced here: 298 us
  Pallas kernels  285 us (95%)
  other arithmetic  6.99 us (2%)
  local copies, waits for them, and re-layouts  5.8 us (2%)
    pallas_call x1, Pallas kernels, updated(): pl.pallas_call(functools.partial(update_kernel, count, factor, head), out...  182 us
    pallas_call x1, Pallas kernels, summed_share(): pl.pallas_call(functools.partial(share_kernel, count, wide), out_shape=(j...  103 us
    convert_element_type x1, other arithmetic, per_device(): base = nesterov.astype(jnp.bfloat16)  6.99 us

profile of v2, /device:TPU:0, one launch (start us, length us, event | category | flops | bytes accessed | tf_op | source)
XLA Modules:
  0.0 298.3 jit_solution(11027365541246762020)
XLA Ops:
  0.6 7.0 %fusion = (bf16[896,1536]{1,0:T(8,128)(2,1)S(1)}, f32[896,1536]{1,0:T(8,128)}) fusion(bf16[896,1536]{1,0:T(8,128)(2,1)} %param.2, f32[896,1536]{1,0:T(8,128)} %param.3), kind=kLoop, calls=%fused_computation.2 | loop fusion | flops 8257536 | bytes 16515072 | tf_op jit(solution)/shard_map/convert_element_type | solution.py:879
  7.6 103.2 %summed_share.1 = (bf16[112,1920]{1,0:T(8,128)(2,1)S(1)}, bf16[384,3584]{1,0:T(8,128)(2,1)S(1)}) custom-call(bf16[7,128,1536]{2,1,0:T(8,128)(2,1)S(1)} %bitcast.1), custom_call_target="tpu_custom_call" | custom-call | tf_op jit(solution)/shard_map/summed_share/pallas_call | solution.py:439
  110.9 0.0 copy-start
  110.9 1.5 copy-done
  112.4 0.0 copy-start.1
  112.4 0.8 copy-done.1
  113.2 181.7 %updated.1 = bf16[896,1536]{1,0:T(8,128)(2,1)} custom-call(bf16[112,1920]{1,0:T(8,128)(2,1)} %copy-done.1, bf16[384,3584]{1,0:T(8,128)(2,1)} %copy-done), custom_call_target="tpu_custom_call" | custom-call | tf_op jit(solution)/shard_map/updated/pallas_call | solution.py:847
  294.8 3.5 %copy.5 = bf16[896,1536]{1,0:T(8,128)(2,1)} copy(bf16[896,1536]{1,0:T(8,128)(2,1)} %updated.1) | data formatting | bytes 5505024
Async XLA Ops:
  110.9 1.5 copy-start
  112.4 0.8 copy-start.1

commit v3 on v2

--- a/solution.py
+++ b/solution.py
@@ -310,156 +310,189 @@
     )
 
 
-def share_kernel(
-    count, wide, base_ref, share_ref, slab_ref, panel, partial, landed, running,
+def sum_share(
+    count, wide, base_ref, slab, gram, partial, share, running_rows,
     panel_send, panel_recv, own_sem, ring_send, ring_recv,
 ):
-    chunks = panel.shape[1]
-    block = chunks * LANES
+    block, width = base_ref.shape
+    chunks = block // LANES
     strip = block // count
-    width = panel.shape[3] // 4
+    half = LANES // 2
+    slab_width = width // 4
     me, column = lax.axis_index("row"), lax.axis_index("col")
-    core = lax.rem(me, 2)
+    chip, core = lax.div(me, 2), lax.rem(me, 2)
     place = ring_place(column, count)
     sign = 1 - 2 * core
     ways = (sign, -sign)
-    meet(
-        pltpu.get_barrier_semaphore(),
-        [{"col": ring_column(place + way, count)} for way in ways]
-        + [{"row": flipped(me, 1)}, {"row": flipped(me, 2)}],
-    )
-
-    def pass_on(slot, source, chunk):
+
+    def panel(slot, chunk, part=None):
+        start = (slot * chunks + chunk) * LANES
+        if part is None:
+            return gram.at[pl.ds(pl.multiple_of(start, LANES), LANES), pl.ds(0, width)]
+        start = pl.multiple_of(start + part * half, half)
+        return gram.at[pl.ds(start, half), pl.ds(0, width)]
+
+    def move(kind, chunk, source, target, bits):
         return remote(
-            source,
-            panel.at[slot, chunk],
-            panel_send.at[slot - 1, chunk],
-            panel_recv.at[slot - 1, chunk],
-            {"row": flipped(me, 2 if slot == 2 else 1)},
-        )
-
-    own = pltpu.make_async_copy(base_ref, panel.at[0], own_sem)
+            source, target, panel_send.at[kind, chunk], panel_recv.at[kind, chunk],
+            {"row": flipped(me, bits)},
+        )
+
+    def to_partner(chunk):
+        rows = pl.ds(chunk * LANES, LANES)
+        return move(0, chunk, base_ref.at[rows], panel(1, chunk), 1)
+
+    def across(j, chunk, own=False):
+        source = panel(1, chunk, core)
+        if own:
+            source = base_ref.at[pl.ds(pl.multiple_of(chunk * LANES + core * half, half), half)]
+        return move(1 + j, chunk, source, panel(2 + j, chunk, core), 2)
+
+    def beside(j, chunk, part):
+        held = panel(2 + j, chunk, part)
+        return move(3 + j, chunk, held, held, 1)
+
+    own = pltpu.make_async_copy(base_ref, gram.at[pl.ds(0, block), pl.ds(0, width)], own_sem)
     own.start()
     for chunk in range(chunks):
-        pass_on(2, base_ref.at[chunk], chunk).start()
-        pass_on(1, base_ref.at[chunk], chunk).start()
+        to_partner(chunk).start()
+
+    for k in range(2):
+        @pl.when(core == k)
+        def _():
+            for j in range(2):
+                for chunk in range(chunks):
+                    if j != k:
+                        to_partner(chunk).wait_recv()
+                    across(j, chunk, j == k).start()
+
     own.wait()
+    piece = ring_send.shape[0]
+    first_half = (chunks + 1) // 2 * 2 * LANES
+    starts = [0, first_half // 2]
+    rest = wide * LANES - first_half
+    step_lanes = pl.cdiv(rest // LANES, 4) * LANES
+    starts += list(range(first_half, wide * LANES, step_lanes))
+    stops = starts[1:] + [wide * LANES]
+    lanes = [pl.ds(start, stop - start) for start, stop in zip(starts, stops)]
+    assert len(lanes) <= piece
+    early, late = range(2), range(2, len(lanes))
+
+    def strip_at(spot):
+        spot = lax.rem(spot + 2 * count, count)
+        return pl.ds(pl.multiple_of(spot * strip, 16), strip)
+
+    def held_at(first, step, k):
+        rows = pl.ds(pl.multiple_of(first + step * strip, 16), strip)
+        return gram.at[rows, pl.ds(width + lanes[k].start, lanes[k].size)]
+
+    def ring_copy(step, k, source):
+        return remote(
+            source, held_at(block, step, k), ring_send.at[k, step], ring_recv.at[k, step],
+            {"col": ring_column(place + ways[k % 2], count)},
+        )
+
+    def ring_start(streams):
+        for k in streams:
+            ring_copy(0, k, partial.at[strip_at(place - ways[k % 2]), lanes[k]]).start()
+
+    def ring_step(step, streams):
+        for k in streams:
+            landed, running = held_at(block, step, k), held_at(running_rows, step, k)
+            ring_copy(step, k, landed).wait_recv()
+            mine = partial[strip_at(place - ways[k % 2] * (step + 2)), lanes[k]]
+            value = landed[...].astype(jnp.float32) + mine.astype(jnp.float32)
+            value = value.astype(jnp.bfloat16)
+
+            @pl.when(step < count - 2)
+            def _():
+                running[...] = value
+                ring_copy(step + 1, k, running).start()
+
+            @pl.when(step == count - 2)
+            def _():
+                share[:, lanes[k]] = value
 
     @pl.loop(0, 4 * chunks)
     def _(event):
-        far = event >= 2 * chunks
-        late = lax.max(event - 2 * chunks, 0)
-        slot = jnp.where(far, 2 + lax.rem(late, 2), lax.div(event, chunks))
-        chunk = jnp.where(far, lax.div(late, 2), lax.rem(event, chunks))
-        for x in range(1, 4):
-            @pl.when(slot == x)
+        slot, chunk = lax.div(event, chunks), lax.rem(event, chunks)
+        for j in range(2):
+            @pl.when(slot == 2 + j)
             def _():
-                pass_on(x, panel.at[2 if x == 3 else 0, chunk], chunk).wait_recv()
-                if x == 2:
-                    pass_on(3, panel.at[2, chunk], chunk).start()
-
-        turned = lax.rem(slot, 2)
-        offset = jnp.where(
-            slot == 2, 2, turned * (2 - (1 - 2 * core) * (2 - slot))
-        )
-        owner = lax.rem(me + offset, 4)
-        piece = panel[slot, chunk]
+                across(j, chunk).wait_recv()
+                beside(j, chunk, core).start()
+
+        @pl.when(event == 2 * chunks)
+        def _():
+            @pl.when(core == 0)
+            def _():
+                ring_start(early)
+
+        @pl.when(event == 3 * chunks)
+        def _():
+            @pl.when(core == 0)
+            def _():
+                ring_start(late)
+
+            @pl.when(core == 1)
+            def _():
+                ring_start(early)
+
+        for j in range(2):
+            @pl.when(slot == 2 + j)
+            def _():
+                beside(j, chunk, 1 - core).wait_recv()
+
+        rows = pl.ds(pl.multiple_of(event * LANES, LANES), LANES)
+        partner_row = 2 * chip + 1 - core
+        far_row = 2 * (1 - chip) + slot - 2
+        owner = jnp.where(slot == 0, me, jnp.where(slot == 1, partner_row, far_row))
         target = pl.ds(pl.multiple_of((owner * chunks + chunk) * LANES, LANES), LANES)
-        mine = pl.ds(pl.multiple_of(me * width, LANES), width)
-        slab_ref[:, target] = panel[slot, chunk, :, mine].T
-        spot = offset * chunks + chunk
-
-        @pl.when(spot < chunks + wide - 1)
+        mine = pl.ds(pl.multiple_of(me * slab_width, LANES), slab_width)
+        slab[:, target] = gram[rows, mine].T
+        skipped = jnp.where(core == 0, slot == 3, slot == 1)
+        spot = chunk + chunks * jnp.where(core == 0, slot, lax.max(slot - 1, 0))
+
+        @pl.when(jnp.logical_not(skipped))
         def _():
-            value = outer_rows(panel[0].reshape(block, panel.shape[3]), piece)
+            value = outer_rows(gram[0:block, 0:width], gram[rows, 0:width])
             value = value.astype(jnp.bfloat16)
             for i in range(chunks):
                 place_in = spot - i
 
                 @pl.when((place_in >= 0) & (place_in < wide))
                 def _():
-                    lanes = pl.ds(pl.multiple_of(place_in * LANES, LANES), LANES)
+                    into = pl.ds(pl.multiple_of(place_in * LANES, LANES), LANES)
                     held = slice(i * LANES, (i + 1) * LANES)
-                    partial[held, lanes] = value[held]
-
-    for slot in range(1, 4):
+                    partial[held, into] = value[held]
+
+        @pl.when(jnp.where(core == 0, slot == 2, slot == 3))
+        def _():
+            ring_step(chunk, early)
+
+        @pl.when(jnp.where(core == 0, slot == 3, False))
+        def _():
+            ring_step(chunk, late)
+
+    @pl.when(core == 1)
+    def _():
+        ring_start(late)
+
+        @pl.loop(0, count - 1)
+        def _(step):
+            ring_step(step, late)
+
+    def sent():
         for chunk in range(chunks):
-            pass_on(slot, panel.at[2 if slot == 3 else 0, chunk], chunk).wait_send()
-
-    size = landed.shape[3]
-    lanes = [
-        pl.ds(start, min(size, wide * LANES - start))
-        for start in range(0, wide * LANES, size)
-    ]
-
-    def strip_at(spot):
-        spot = lax.rem(spot + 2 * count, count)
-        return pl.ds(pl.multiple_of(spot * strip, 16), strip)
-
-    def ring_copy(step, k, source):
-        return remote(
-            source,
-            landed.at[k, step, :, pl.ds(0, lanes[k].size)],
-            ring_send.at[k, step],
-            ring_recv.at[k, step],
-            {"col": ring_column(place + ways[k % 2], count)},
-        )
-
-    copies = []
-    for k in range(len(lanes)):
-        source = partial.at[strip_at(place - ways[k % 2]), lanes[k]]
-        copies.append(ring_copy(0, k, source))
-        copies[k].start()
-    sent = list(copies)
-    for step in range(count - 1):
-        for k in range(len(lanes)):
-            held = pl.ds(0, lanes[k].size)
-            copies[k].wait_recv()
-            mine = partial[strip_at(place - ways[k % 2] * (step + 2)), lanes[k]]
-            value = landed[k, step, :, held].astype(jnp.float32) + mine.astype(jnp.float32)
-            value = value.astype(jnp.bfloat16)
-            if step < count - 2:
-                running[k, step, :, held] = value
-                copies[k] = ring_copy(step + 1, k, running.at[k, step, :, held])
-                copies[k].start()
-                sent.append(copies[k])
-            else:
-                share_ref[:, lanes[k]] = value
-    for copy in sent:
-        copy.wait_send()
-
-
-def summed_share(base, count, wide):
-    block, width = base.shape
-    strip = block // count
-    chunks = block // LANES
-    streams = 4
-    piece = pl.cdiv(wide, streams) * LANES
-    vmem = pl.BlockSpec(memory_space=pltpu.VMEM)
-    return pl.pallas_call(
-        functools.partial(share_kernel, count, wide),
-        out_shape=(
-            jax.ShapeDtypeStruct((strip, wide * LANES), jnp.bfloat16),
-            jax.ShapeDtypeStruct((width // 4, 4 * block), jnp.bfloat16),
-        ),
-        in_specs=[pl.BlockSpec(memory_space=pl.ANY)],
-        out_specs=(vmem, vmem),
-        scratch_shapes=[
-            pltpu.VMEM((4, chunks, LANES, width), jnp.bfloat16),
-            pltpu.VMEM((block, wide * LANES), jnp.bfloat16),
-            pltpu.VMEM((streams, count - 1, strip, piece), jnp.bfloat16),
-            pltpu.VMEM((streams, count - 1, strip, piece), jnp.bfloat16),
-            pltpu.SemaphoreType.DMA((3, chunks)),
-            pltpu.SemaphoreType.DMA((3, chunks)),
-            pltpu.SemaphoreType.DMA,
-            pltpu.SemaphoreType.DMA((streams, count - 1)),
-            pltpu.SemaphoreType.DMA((streams, count - 1)),
-        ],
-        compiler_params=pltpu.CompilerParams(
-            collective_id=1, has_side_effects=True, vmem_limit_bytes=48 * 1024 * 1024
-        ),
-        name="summed_share",
-    )(base.reshape(chunks, LANES, width))
+            to_partner(chunk).wait_send()
+            for j in range(2):
+                across(j, chunk).wait_send()
+                beside(j, chunk, core).wait_send()
+        for step in range(count - 1):
+            for k in range(len(lanes)):
+                ring_copy(step, k, held_at(running_rows, step, k)).wait_send()
+
+    return sent
 
 
 def gather_plan(count):
@@ -612,13 +645,14 @@
 
 
 def update_kernel(
-    count, factor, head, share_ref, slab_ref, out_ref, gram, land, first, rough, exact,
-    stage, total, sends, recvs, own_sem, free_sem, out_send, out_recv,
+    count, factor, head, base_ref, out_ref, gram, land, slab_ref, first, rough, exact,
+    stage, total, partial, sends, recvs, own_sem, free_sem, out_send, out_recv,
+    panel_send, panel_recv, ring_send, ring_recv,
 ):
     size = gram.shape[0]
     blocks = size // LANES
-    strip, reach = share_ref.shape
-    wide = reach // LANES
+    strip = size // 4 // count
+    wide = land.shape[1] // LANES
     width = slab_ref.shape[0]
     tile = 512 if size % 512 == 0 else LANES
     block = size // 4
@@ -676,9 +710,10 @@
             def _():
                 place_block(row * chunks + spot, squares)
 
-    own = pltpu.make_async_copy(share_ref, land.at[mine_rows], own_sem)
-    own.start()
-    own.wait()
+    summed_out = sum_share(
+        count, wide, base_ref, slab_ref, gram, partial, land.at[mine_rows],
+        block + strip * count, panel_send, panel_recv, own_sem, ring_send, ring_recv,
+    )
     total[...] = jnp.zeros_like(total)
 
     def run_groups(groups, steps, squares):
@@ -697,6 +732,7 @@
 
     steps = gather_steps(count, head, strip, land, sends.at[0], recvs.at[0])
     steps[0]()
+    summed_out()
     run_groups(gather_groups(count, 4), steps, True)
     for target in near:
         pl.semaphore_signal(
@@ -706,8 +742,8 @@
     scale = 1.0 / jnp.sqrt(jnp.sqrt(quartic) + EPSILON)
     square = scale * scale
 
-    def times_gram(source, finish, hooks=()):
-        @pl.loop(0, size // tile)
+    def times_gram(source, finish, hooks=(), begin=0, tiles=size // tile):
+        @pl.loop(0, tiles)
         def _(step):
             for k, calls in enumerate(hooks):
                 if calls:
@@ -716,7 +752,8 @@
                         for call in calls:
                             call()
 
-            columns = pl.ds(pl.multiple_of(step * tile, tile), tile)
+            at = lax.rem(begin + step, size // tile)
+            columns = pl.ds(pl.multiple_of(at * tile, tile), tile)
             finish(
                 columns,
                 jnp.dot(source[...], gram[:, columns], preferred_element_type=jnp.float32),
@@ -749,7 +786,12 @@
     times_gram(mine, after_square)
     times_gram(left, after_cube)
     times_gram(right, after_third)
-    times_gram(left, after_cube)
+    times_gram(
+        left,
+        after_cube,
+        begin=lax.div(number * strip, tile),
+        tiles=min(size // tile, pl.cdiv((wide + 1) * LANES, tile) + 1),
+    )
 
     pl.semaphore_wait(free_sem, len(near))
     for group in range(strip // 16):
@@ -796,79 +838,95 @@
     times_gram(rough, combine, paced[slots:])
     run_groups(groups, steps, False)
 
-    def after_product(columns, value):
-        exact[:, columns] = (
-            COEF_LINEAR * first[:, columns].astype(jnp.float32) + COEF_CUBIC * value
-        )
-        rough[:, columns] = value.astype(jnp.bfloat16)
-
-    times_gram(first, after_product)
+    def out_copy(bits, part):
+        lanes = pl.ds(pl.multiple_of(me * width + part * LANES, LANES), LANES)
+        held = pl.ds(pl.multiple_of(part * LANES, LANES), LANES)
+        return remote(
+            stage.at[bits, :, held],
+            out_ref.at[:, lanes],
+            out_send.at[bits - 1, part],
+            out_recv.at[bits - 1, part],
+            {"row": flipped(me, bits)},
+        )
+
+    @pl.loop(0, width // LANES)
+    def _(index):
+        part = pl.ds(pl.multiple_of(index * LANES, LANES), LANES)
+
+        def after_product(columns, value):
+            exact[part, columns] = (
+                COEF_LINEAR * first[part, columns].astype(jnp.float32) + COEF_CUBIC * value
+            )
+            rough[part, columns] = value.astype(jnp.bfloat16)
+
+        times_gram(first.at[part], after_product)
+
+        @pl.loop(0, 4)
+        def _(step):
+            bits = 3 - step
+            chip, core = lax.div(me, 2), lax.rem(me, 2)
+            high, low = lax.div(bits, 2), lax.rem(bits, 2)
+            owner = 2 * (chip + high - 2 * chip * high) + (core + low - 2 * core * low)
+            columns = pl.ds(pl.multiple_of(owner * block, LANES), block)
+            value = jnp.dot(
+                rough[part, :], gram[:, columns], preferred_element_type=jnp.float32
+            )
+            value = (exact[part, columns] + COEF_QUINTIC * value) * (scale * factor)
+            stage[bits, :, part] = value.astype(jnp.bfloat16).T
+            for x in range(1, 4):
+                @pl.when(bits == x)
+                def _():
+                    out_copy(x, index).start()
 
     lanes = pl.ds(pl.multiple_of(me * width, LANES), width)
-
-    def out_copy(bits):
-        return remote(
-            stage.at[bits],
-            out_ref.at[:, lanes],
-            out_send.at[bits - 1],
-            out_recv.at[bits - 1],
-            {"row": flipped(me, bits)},
-        )
-
-    @pl.loop(0, 4)
-    def _(step):
-        bits = 3 - step
-        chip, core = lax.div(me, 2), lax.rem(me, 2)
-        high, low = lax.div(bits, 2), lax.rem(bits, 2)
-        owner = 2 * (chip + high - 2 * chip * high) + (core + low - 2 * core * low)
-        columns = pl.ds(pl.multiple_of(owner * block, LANES), block)
-        value = jnp.dot(rough[...], gram[:, columns], preferred_element_type=jnp.float32)
-        value = (exact[:, columns] + COEF_QUINTIC * value) * (scale * factor)
-        stage[bits] = value.astype(jnp.bfloat16).T
-        for x in range(1, 4):
-            @pl.when(bits == x)
-            def _():
-                out_copy(x).start()
-
     kept = pltpu.make_async_copy(stage.at[0], out_ref.at[:, lanes], own_sem)
     kept.start()
     kept.wait()
     for bits in range(1, 4):
-        out_copy(bits).wait()
-
-
-def updated(share, slab, factor, count, wide):
-    width, size = slab.shape
-    strip = share.shape[0]
+        for part in range(width // LANES):
+            out_copy(bits, part).wait()
+
+
+def updated(base, factor, count, wide):
+    block, full_width = base.shape
+    size, width = 4 * block, full_width // 4
+    strip = block // count
     head = strip * 4 // 7 // 16 * 16
-    vmem = pl.BlockSpec(memory_space=pltpu.VMEM)
+    chunks = block // LANES
     half = pltpu.VMEM((width, size), jnp.bfloat16)
     messages = len(gather_names(count))
+    dma = pltpu.SemaphoreType.DMA
     return pl.pallas_call(
         functools.partial(update_kernel, count, factor, head),
-        out_shape=jax.ShapeDtypeStruct((size // 4, 4 * width), jnp.bfloat16),
-        in_specs=[vmem, vmem],
+        out_shape=jax.ShapeDtypeStruct((block, full_width), jnp.bfloat16),
+        in_specs=[pl.BlockSpec(memory_space=pl.ANY)],
         out_specs=pl.BlockSpec(memory_space=pl.ANY),
         scratch_shapes=[
             pltpu.VMEM((size, size), jnp.bfloat16),
             pltpu.VMEM((size, wide * LANES), jnp.bfloat16),
             half,
             half,
+            half,
             pltpu.VMEM((width, size), jnp.float32),
-            pltpu.VMEM((4, size // 4, width), jnp.bfloat16),
+            pltpu.VMEM((4, block, width), jnp.bfloat16),
             pltpu.VMEM((8, LANES), jnp.float32),
-            pltpu.SemaphoreType.DMA((2, messages)),
-            pltpu.SemaphoreType.DMA((2, messages)),
-            pltpu.SemaphoreType.DMA,
+            pltpu.VMEM((block, wide * LANES), jnp.bfloat16),
+            dma((2, messages)),
+            dma((2, messages)),
+            dma,
             pltpu.SemaphoreType.REGULAR,
-            pltpu.SemaphoreType.DMA((3,)),
-            pltpu.SemaphoreType.DMA((3,)),
+            dma((3, width // LANES)),
+            dma((3, width // LANES)),
+            dma((5, chunks)),
+            dma((5, chunks)),
+            dma((6, count - 1)),
+            dma((6, count - 1)),
         ],
         compiler_params=pltpu.CompilerParams(
-            collective_id=2, has_side_effects=True, vmem_limit_bytes=63 * 1024 * 1024
+            collective_id=1, has_side_effects=True, vmem_limit_bytes=63 * 1024 * 1024
         ),
         name="updated",
-    )(share, slab)
+    )(base)
 
 
 def per_device(factor, gradient, momentum):
@@ -890,10 +948,10 @@
         and strip % 16 == 0
         and 32 <= strip < LANES
         and block // LANES + 1 == count
+        and base.shape[1] + (2 * block // LANES + 1) * LANES <= 4 * block
     ):
         wide = 4 * block // LANES // 2 + 1
-        share, slab = summed_share(base, count, wide)
-        return (updated(share, slab, factor, count, wide), buffer)
+        return (updated(base, factor, count, wide), buffer)
     half = block // 2
     middle = rows // 2
     me = lax.axis_index("row")

time: 299 us -> 271 us (0.906)
  Pallas kernels: 285 us -> 259 us
    pallas_call x1 -> x0, Pallas kernels: 103 us -> none  [summed_share(): pl.pallas_call(functools.partial(share_kernel, count, wide), out_shape=(j...]
    pallas_call x1, Pallas kernels: 182 us -> 259 us  [updated(): pl.pallas_call(functools.partial(update_kernel, count, factor, head), out...]
where the time goes in v3:
time: 271 us
  Pallas kernels  259 us (96%)
  other arithmetic  7.89 us (3%)
  local copies, waits for them, and re-layouts  3.49 us (1%)
    pallas_call x1, Pallas kernels, updated(): pl.pallas_call(functools.partial(update_kernel, count, factor, head), out...  259 us
    convert_element_type x1, other arithmetic, per_device(): base = nesterov.astype(jnp.bfloat16)  7.89 us

profile of v3, /device:TPU:0, one launch (start us, length us, event | category | flops | bytes accessed | tf_op | source)
XLA Modules:
  0.0 270.8 jit_solution(6017801885344623022)
XLA Ops:
  0.6 7.9 %fusion = (bf16[896,1536]{1,0:T(8,128)(2,1)}, f32[896,1536]{1,0:T(8,128)}) fusion(bf16[896,1536]{1,0:T(8,128)(2,1)} %param.2, f32[896,1536]{1,0:T(8,128)} %param.3), kind=kLoop, calls=%fused_computation.2 | loop fusion | flops 8257536 | bytes 16515072 | tf_op jit(solution)/shard_map/convert_element_type | solution.py:937
  8.5 258.8 %updated.1 = bf16[896,1536]{1,0:T(8,128)(2,1)} custom-call(bf16[896,1536]{1,0:T(8,128)(2,1)} %get-tuple-element.2.base_ref), custom_call_target="tpu_custom_call" | custom-call | tf_op jit(solution)/shard_map/updated/pallas_call | solution.py:899
  267.3 3.5 %copy.5 = bf16[896,1536]{1,0:T(8,128)(2,1)} copy(bf16[896,1536]{1,0:T(8,128)(2,1)} %updated.1) | data formatting | bytes 5505024

commit v4 on v3

--- a/solution.py
+++ b/solution.py
@@ -810,7 +810,7 @@
     paced = [[] for _ in range(2 * slots)]
     early, waiting = [], []
     for k, (events, works) in enumerate(groups):
-        if len(early) + len(events) <= 18:
+        if len(early) + len(events) <= 20:
             early += events
             waiting += works
             groups[k] = ([], [])
@@ -818,7 +818,7 @@
             groups[k] = (events, waiting + works)
             break
     for k, name in enumerate(early):
-        paced[min(2 * slots - 1, k * 2 * slots // len(early))].append(
+        paced[slots // 2 + k * (2 * slots - slots // 2) // len(early)].append(
             functools.partial(steps[1], name)
         )
 

time: 271 us -> 269 us (level)
  no operation moved by 1% of the time
where the time goes in v4:
time: 269 us
  Pallas kernels  257 us (96%)
  other arithmetic  7.89 us (3%)
  local copies, waits for them, and re-layouts  3.49 us (1%)
    pallas_call x1, Pallas kernels, updated(): pl.pallas_call(functools.partial(update_kernel, count, factor, head), out...  257 us
    convert_element_type x1, other arithmetic, per_device(): base = nesterov.astype(jnp.bfloat16)  7.89 us

profile of v4, /device:TPU:0, one launch (start us, length us, event | category | flops | bytes accessed | tf_op | source)
XLA Modules:
  0.0 268.9 jit_solution(16071430356369432774)
XLA Ops:
  0.6 7.9 %fusion = (bf16[896,1536]{1,0:T(8,128)(2,1)}, f32[896,1536]{1,0:T(8,128)}) fusion(bf16[896,1536]{1,0:T(8,128)(2,1)} %param.2, f32[896,1536]{1,0:T(8,128)} %param.3), kind=kLoop, calls=%fused_computation.2 | loop fusion | flops 8257536 | bytes 16515072 | tf_op jit(solution)/shard_map/convert_element_type | solution.py:937
  8.5 256.8 %updated.1 = bf16[896,1536]{1,0:T(8,128)(2,1)} custom-call(bf16[896,1536]{1,0:T(8,128)(2,1)} %get-tuple-element.2.base_ref), custom_call_target="tpu_custom_call" | custom-call | tf_op jit(solution)/shard_map/updated/pallas_call | solution.py:899
  265.4 3.5 %copy.5 = bf16[896,1536]{1,0:T(8,128)(2,1)} copy(bf16[896,1536]{1,0:T(8,128)(2,1)} %updated.1) | data formatting | bytes 5505024

commit v5 on v4

--- a/solution.py
+++ b/solution.py
@@ -733,7 +733,7 @@
     steps = gather_steps(count, head, strip, land, sends.at[0], recvs.at[0])
     steps[0]()
     summed_out()
-    run_groups(gather_groups(count, 4), steps, True)
+    run_groups(gather_groups(count, 3), steps, True)
     for target in near:
         pl.semaphore_signal(
             free_sem, inc=1, device_id=target, device_id_type=pl.DeviceIdType.MESH
@@ -805,12 +805,12 @@
 
     steps = gather_steps(count, head, strip, land, sends.at[1], recvs.at[1])
     steps[0]()
-    groups = gather_groups(count, 4)
+    groups = gather_groups(count, 3)
     slots = size // tile
     paced = [[] for _ in range(2 * slots)]
     early, waiting = [], []
     for k, (events, works) in enumerate(groups):
-        if len(early) + len(events) <= 20:
+        if len(early) + len(events) <= 21:
             early += events
             waiting += works
             groups[k] = ([], [])

time: 269 us -> 270 us (level)
  no operation moved by 1% of the time
where the time goes in v5:
time: 270 us
  Pallas kernels  258 us (96%)
  other arithmetic  7.89 us (3%)
  local copies, waits for them, and re-layouts  3.49 us (1%)
    pallas_call x1, Pallas kernels, updated(): pl.pallas_call(functools.partial(update_kernel, count, factor, head), out...  258 us
    convert_element_type x1, other arithmetic, per_device(): base = nesterov.astype(jnp.bfloat16)  7.89 us

profile of v5, /device:TPU:0, one launch (start us, length us, event | category | flops | bytes accessed | tf_op | source)
XLA Modules:
  0.0 270.1 jit_solution(1018948255776344030)
XLA Ops:
  0.6 7.9 %fusion = (bf16[896,1536]{1,0:T(8,128)(2,1)}, f32[896,1536]{1,0:T(8,128)}) fusion(bf16[896,1536]{1,0:T(8,128)(2,1)} %param.2, f32[896,1536]{1,0:T(8,128)} %param.3), kind=kLoop, calls=%fused_computation.2 | loop fusion | flops 8257536 | bytes 16515072 | tf_op jit(solution)/shard_map/convert_element_type | solution.py:937
  8.5 258.1 %updated.1 = bf16[896,1536]{1,0:T(8,128)(2,1)} custom-call(bf16[896,1536]{1,0:T(8,128)(2,1)} %get-tuple-element.2.base_ref), custom_call_target="tpu_custom_call" | custom-call | tf_op jit(solution)/shard_map/updated/pallas_call | solution.py:899
  266.6 3.5 %copy.5 = bf16[896,1536]{1,0:T(8,128)(2,1)} copy(bf16[896,1536]{1,0:T(8,128)(2,1)} %updated.1) | data formatting | bytes 5505024
